TPU v7x, 256 devices: a whole 4x4x8 slice. The times are simulated.
256 devices in a mesh: front: 8 (over z), row: 32 (over x, y, core).
Axes of the slice: x: 4, y: 4, z: 8, core: 2. Of those that a mesh axis runs over, the one named last changes fastest.
Arguments:
- panels: bfloat16 [8, 4096, 1280], P('front', 'row'), may hold values from -6 to 6
- reflectors: bfloat16 [8, 4096, 512], P('front', 'row'), may hold values from -6 to 6
- block_coeffs: bfloat16 [8, 512, 512], P('front')
- block_mask: int32 [8, 32, 4], P('front', 'row'), may hold values 0 or 1
- block_starts: int32 [8, 4], P('front'), may hold values from 0 to 2048, as said below
- carry_map: int32 [8, 1024], P('front'), may hold values from 0 to 4095, as said below
Outputs:
- panels_out: bfloat16 [8, 4096, 1280], P('front', 'row')
Inputs may be any that keep to these rules, and one draw needn't show every extreme that they name: `block_starts`: nondecreasing along the reflector blocks of a front. `carry_map`: within a front the targets are distinct, and carried row i lands in the 128-row block number i % 32, which receives exactly 32 carried rows, its last row among them.
All inputs are finite; a program needn't handle non-finite values. No bound on the sum of `block_mask` on one device may be relied on, other than what follows from the above.
Results may differ from a plain program's by a relative error of at most 0.017.
Values may be sent and summed in bfloat16 or wider, within the bound.
No kernel may reach another device: no remote copies, remote signals or barrier semaphores. Data moves between devices by JAX's collectives and lax.ppermute only.
A program may use at most 64 MiB of HBM per device.

v0:
```python
import jax
import jax.numpy as jnp
from jax import lax
from jax.sharding import PartitionSpec as P

PW = 256
NPANEL = 5


def from_behind(value, axis, steps):
    count = lax.axis_size(axis)
    initial, last = (max(0, -steps), min(count, count - steps))
    return lax.ppermute(value, axis, [(source, source + steps) for source in range(initial, last)])


def spread_rows(pieces):
    return lax.all_to_all(pieces, "row", split_axis=1, concat_axis=1, tiled=True)


def pass_along(pieces):
    return from_behind(pieces, "front", 1)


def local(panels, reflectors, block_coeffs, block_mask, block_starts, carry_map):
    row_count = lax.axis_size("row")
    front_count = lax.axis_size("front")
    row_index = lax.axis_index("row")
    front_index = lax.axis_index("front")
    row_span = panels.shape[1]
    tail_start = 3 * row_count // 4
    quarter = row_count - tail_start
    per_source = row_span // row_count
    global_rows = row_index * row_span + jnp.arange(row_span, dtype=jnp.int32)
    mask_full = jnp.repeat(jnp.repeat(block_mask[0], 128, axis=0), 128, axis=1)
    start_cols = jnp.repeat(block_starts[0], 128)
    retained = (mask_full == 1) & (global_rows[:, None] >= start_cols[None, :])
    effective = jnp.where(retained, reflectors[0], jnp.zeros_like(reflectors[0]))
    coeffs = block_coeffs[0]
    target_table = carry_map[0].reshape(quarter, per_source, row_count)
    own_targets = lax.dynamic_slice_in_dim(target_table, row_index, 1, 2)[:, :, 0]
    local_target = (own_targets.T - row_index * row_span).reshape(-1)
    placement = (jnp.arange(row_span, dtype=jnp.int32)[:, None] == local_target[None, :]).astype(
        jnp.bfloat16
    )
    is_tail = row_index >= tail_start
    initial = jnp.zeros((per_source, row_count, PW), jnp.bfloat16)

    def advance(step_index, state):
        out_buffer, incoming = state
        panel_index = step_index - front_index
        is_live = (panel_index >= 0) & (panel_index < NPANEL)
        panel_pos = jnp.clip(panel_index, 0, NPANEL - 1) * PW
        received = spread_rows(incoming)[:, tail_start:, :]
        moved = jnp.dot(
            placement, received.reshape(row_span // 4, PW), preferred_element_type=jnp.float32
        )
        own_panel = lax.dynamic_slice_in_dim(panels[0], panel_pos, PW, 1)
        assembled = (own_panel.astype(jnp.float32) + moved).astype(jnp.bfloat16)
        partial_value = lax.dot_general(
            effective, assembled, (((0,), (0,)), ((), ())), preferred_element_type=jnp.float32
        )
        totals = lax.psum(partial_value, "row")
        mixed = lax.dot_general(
            coeffs,
            totals.astype(jnp.bfloat16),
            (((0,), (0,)), ((), ())),
            preferred_element_type=jnp.float32,
        ).astype(jnp.bfloat16)
        result = (
            assembled.astype(jnp.float32)
            - jnp.dot(effective, mixed, preferred_element_type=jnp.float32)
        ).astype(jnp.bfloat16)
        current = lax.dynamic_slice_in_dim(out_buffer, panel_pos, PW, 1)
        out_buffer = lax.dynamic_update_slice_in_dim(
            out_buffer, jnp.where(is_live, result, current), panel_pos, 1
        )
        outgoing = jnp.where(is_tail, result, jnp.zeros_like(result)).reshape(
            per_source, row_count, PW
        )
        following = pass_along(outgoing)
        return (out_buffer, following)

    out_buffer, leftover = lax.fori_loop(
        0, front_count + NPANEL - 1, advance, (jnp.zeros_like(panels[0]), initial)
    )
    return out_buffer[None]


def solution(mesh):
    in_specs = (
        P("front", "row", None),
        P("front", "row", None),
        P("front", None, None),
        P("front", "row", None),
        P("front", None),
        P("front", None),
    )
    out_specs = P("front", "row", None)
    return jax.shard_map(local, mesh=mesh, in_specs=in_specs, out_specs=out_specs, check_vma=False)
```

profile of v0, /device:TPU:225, one launch (start us, length us, event | category | flops | bytes accessed | tf_op | source)
XLA Modules:
  0.0 1805.1 jit_solution(1654952419590082812)
XLA Ops:
  4.1 1800.2 %while.16 = (s32[]{:T(128)}, bf16[128,1280]{1,0:T(8,128)(2,1)S(1)}, bf16[4,32,256]{2,1,0:T(8,128)(2,1)S(1)}, s32[]{:T(128)}, bf16[1,128,1280]{2,1,0:T(8,128)(2,1...) while((s32[]{:T(128)}, bf16[128,1280]{1,0:T(8,128)(2,1)S(1)}, ...), condition=%wide.region_2.3_spmd.clone, body=%wide.region_0.2_spmd.clone.sunk | while | flops 203956240 | bytes 3457478 | solution.py:83
  21.2 124.3 %all-reduce.1 = bf16[512,256]{0,1:T(8,128)(2,1)S(1)} all-reduce(f32[512,256]{0,1:T(8,128)S(1)} %convolution_bitcast_fusion.2), channel_id=1, replica_groups=mesh['front'=8,'row'=32] {'row'}, use_global_device_ids=true, to_apply=%region_1.1 | all-reduce | flops 131072 | bytes 786432 | tf_op jit(solution)/shard_map/while/body/eval_jaxpr/psum | solution.py:62
  151.7 10.4 all-to-all-start
  170.8 124.3 %all-reduce.1 = bf16[512,256]{0,1:T(8,128)(2,1)S(1)} all-reduce(f32[512,256]{0,1:T(8,128)S(1)} %convolution_bitcast_fusion.2), channel_id=1, replica_groups=mesh['front'=8,'row'=32] {'row'}, use_global_device_ids=true, to_apply=%region_1.1 | all-reduce | flops 131072 | bytes 786432 | tf_op jit(solution)/shard_map/while/body/eval_jaxpr/psum | solution.py:62
  301.3 10.4 all-to-all-start
  320.4 124.3 %all-reduce.1 = bf16[512,256]{0,1:T(8,128)(2,1)S(1)} all-reduce(f32[512,256]{0,1:T(8,128)S(1)} %convolution_bitcast_fusion.2), channel_id=1, replica_groups=mesh['front'=8,'row'=32] {'row'}, use_global_device_ids=true, to_apply=%region_1.1 | all-reduce | flops 131072 | bytes 786432 | tf_op jit(solution)/shard_map/while/body/eval_jaxpr/psum | solution.py:62
  450.9 10.4 all-to-all-start
  470.0 124.3 %all-reduce.1 = bf16[512,256]{0,1:T(8,128)(2,1)S(1)} all-reduce(f32[512,256]{0,1:T(8,128)S(1)} %convolution_bitcast_fusion.2), channel_id=1, replica_groups=mesh['front'=8,'row'=32] {'row'}, use_global_device_ids=true, to_apply=%region_1.1 | all-reduce | flops 131072 | bytes 786432 | tf_op jit(solution)/shard_map/while/body/eval_jaxpr/psum | solution.py:62
  600.4 10.4 all-to-all-start
  619.5 124.3 %all-reduce.1 = bf16[512,256]{0,1:T(8,128)(2,1)S(1)} all-reduce(f32[512,256]{0,1:T(8,128)S(1)} %convolution_bitcast_fusion.2), channel_id=1, replica_groups=mesh['front'=8,'row'=32] {'row'}, use_global_device_ids=true, to_apply=%region_1.1 | all-reduce | flops 131072 | bytes 786432 | tf_op jit(solution)/shard_map/while/body/eval_jaxpr/psum | solution.py:62
  750.0 10.4 all-to-all-start
  769.1 124.3 %all-reduce.1 = bf16[512,256]{0,1:T(8,128)(2,1)S(1)} all-reduce(f32[512,256]{0,1:T(8,128)S(1)} %convolution_bitcast_fusion.2), channel_id=1, replica_groups=mesh['front'=8,'row'=32] {'row'}, use_global_device_ids=true, to_apply=%region_1.1 | all-reduce | flops 131072 | bytes 786432 | tf_op jit(solution)/shard_map/while/body/eval_jaxpr/psum | solution.py:62
  900.4 10.1 all-to-all-start
  919.2 124.3 %all-reduce.1 = bf16[512,256]{0,1:T(8,128)(2,1)S(1)} all-reduce(f32[512,256]{0,1:T(8,128)S(1)} %convolution_bitcast_fusion.2), channel_id=1, replica_groups=mesh['front'=8,'row'=32] {'row'}, use_global_device_ids=true, to_apply=%region_1.1 | all-reduce | flops 131072 | bytes 786432 | tf_op jit(solution)/shard_map/while/body/eval_jaxpr/psum | solution.py:62
  1051.2 10.1 all-to-all-start
  1070.0 124.3 %all-reduce.1 = bf16[512,256]{0,1:T(8,128)(2,1)S(1)} all-reduce(f32[512,256]{0,1:T(8,128)S(1)} %convolution_bitcast_fusion.2), channel_id=1, replica_groups=mesh['front'=8,'row'=32] {'row'}, use_global_device_ids=true, to_apply=%region_1.1 | all-reduce | flops 131072 | bytes 786432 | tf_op jit(solution)/shard_map/while/body/eval_jaxpr/psum | solution.py:62
  1202.0 10.1 all-to-all-start
  1220.8 124.3 %all-reduce.1 = bf16[512,256]{0,1:T(8,128)(2,1)S(1)} all-reduce(f32[512,256]{0,1:T(8,128)S(1)} %convolution_bitcast_fusion.2), channel_id=1, replica_groups=mesh['front'=8,'row'=32] {'row'}, use_global_device_ids=true, to_apply=%region_1.1 | all-reduce | flops 131072 | bytes 786432 | tf_op jit(solution)/shard_map/while/body/eval_jaxpr/psum | solution.py:62
  1352.7 10.1 all-to-all-start
  1371.6 124.3 %all-reduce.1 = bf16[512,256]{0,1:T(8,128)(2,1)S(1)} all-reduce(f32[512,256]{0,1:T(8,128)S(1)} %convolution_bitcast_fusion.2), channel_id=1, replica_groups=mesh['front'=8,'row'=32] {'row'}, use_global_device_ids=true, to_apply=%region_1.1 | all-reduce | flops 131072 | bytes 786432 | tf_op jit(solution)/shard_map/while/body/eval_jaxpr/psum | solution.py:62
  1503.5 10.1 all-to-all-start
  1522.3 124.3 %all-reduce.1 = bf16[512,256]{0,1:T(8,128)(2,1)S(1)} all-reduce(f32[512,256]{0,1:T(8,128)S(1)} %convolution_bitcast_fusion.2), channel_id=1, replica_groups=mesh['front'=8,'row'=32] {'row'}, use_global_device_ids=true, to_apply=%region_1.1 | all-reduce | flops 131072 | bytes 786432 | tf_op jit(solution)/shard_map/while/body/eval_jaxpr/psum | solution.py:62
  1654.3 10.1 all-to-all-start
  1673.1 124.3 %all-reduce.1 = bf16[512,256]{0,1:T(8,128)(2,1)S(1)} all-reduce(f32[512,256]{0,1:T(8,128)S(1)} %convolution_bitcast_fusion.2), channel_id=1, replica_groups=mesh['front'=8,'row'=32] {'row'}, use_global_device_ids=true, to_apply=%region_1.1 | all-reduce | flops 131072 | bytes 786432 | tf_op jit(solution)/shard_map/while/body/eval_jaxpr/psum | solution.py:62
  (121 shorter events, 200.5 us)
Async XLA Ops:
  4.8 15.1 all-to-all-start
  146.0 5.0 collective-permute-start
  151.7 17.8 all-to-all-start
  295.6 5.0 collective-permute-start
  301.3 17.8 all-to-all-start
  445.2 5.0 collective-permute-start
  450.9 17.8 all-to-all-start
  594.7 5.0 collective-permute-start
  600.4 17.8 all-to-all-start
  744.3 5.0 collective-permute-start
  750.0 17.8 all-to-all-start
  893.9 5.9 collective-permute-start
  900.4 17.6 all-to-all-start
  1044.0 6.5 collective-permute-start
  1051.2 17.6 all-to-all-start
  1194.8 6.5 collective-permute-start
  1202.0 17.6 all-to-all-start
  1345.6 6.5 collective-permute-start
  1352.7 17.6 all-to-all-start
  1496.3 6.5 collective-permute-start
  1503.5 17.6 all-to-all-start
  1647.1 6.5 collective-permute-start
  1654.3 17.6 all-to-all-start
  1797.9 6.5 collective-permute-start
  (5 other events, 5.5 us)
where the time goes:
time: 1820 us; the launch traced here: 1810 us
  blocking collectives  1490 us (82%)
  waiting for transfers between devices  144 us (8%)
  starting transfers between devices  136 us (7%)
  matrix products  20.5 us (1%)
    psum x12, blocking collectives, advance(): totals = lax.psum(partial_value, 'row')  1490 us
    all_to_all x12, starting transfers between devices, spread_rows(): lax.all_to_all(pieces, 'row', split_axis=1, concat_axis=1, tiled=True)  120 us
    all_to_all x12, waiting for transfers between devices, spread_rows(): lax.all_to_all(pieces, 'row', split_axis=1, concat_axis=1, tiled=True)  89.4 us
    ppermute x12, waiting for transfers between devices, from_behind(): lax.ppermute(value, axis, [(source, source + steps) for source in range(i...  54.3 us
  transfers between devices with their start and end apart: 24, of which 24 were waited for; matrix products, arithmetic and copies ran while one was open for 0% of the time, Pallas kernels for 0%

commit v1 on v0

v1 whole, which is shorter than its diff:
```python
import jax
import jax.numpy as jnp
import numpy as np
from jax import lax
from jax.sharding import PartitionSpec as P

BF = jnp.bfloat16
F32 = jnp.float32


def mm(a, b, dims=((1,), (0,))):
    return lax.dot_general(a, b, (dims, ((), ())), preferred_element_type=F32)


def local(panels, reflectors, block_coeffs, block_mask, block_starts, carry_map):
    rows = lax.axis_size("row")
    fronts = lax.axis_size("front")
    row = lax.axis_index("row")
    front = lax.axis_index("front")
    span, cols = panels.shape[1:]
    width = reflectors.shape[2]
    part = cols // rows
    carried = carry_map.shape[1]
    each = carried // rows
    total = span * rows
    tail = total - carried

    ids = row * span + lax.broadcasted_iota(jnp.int32, (span, width), 0)
    starts = jnp.repeat(block_starts[0], 128)
    kept = (jnp.repeat(block_mask[0, 0], 128)[None, :] == 1) & (ids >= starts[None, :])
    own = jnp.where(kept, reflectors[0], jnp.zeros_like(reflectors[0]))
    eff = lax.all_gather(own, "row", axis=0, tiled=True)

    pieces = panels[0].T.reshape(rows, part, span)
    got = lax.all_to_all(pieces, "row", 0, 0, tiled=True)
    pan = got.transpose(1, 0, 2).reshape(part, total)

    targets = carry_map[0].reshape(each, rows).T
    offsets = targets - span * jnp.arange(rows, dtype=jnp.int32)[:, None]
    pick = (offsets[:, :, None] == jnp.arange(span, dtype=jnp.int32)).astype(BF)
    gath = lax.dot_general(
        pick, eff.reshape(rows, span, width), (((2,), (1,)), ((0,), (0,))), preferred_element_type=F32
    ).astype(BF).reshape(carried, width)
    low = eff[tail:].reshape(each, rows, width).transpose(1, 0, 2).reshape(carried, width)
    order = (jnp.arange(carried, dtype=jnp.int32) % each) * rows + jnp.arange(carried, dtype=jnp.int32) // each
    swap = (jnp.arange(carried, dtype=jnp.int32)[:, None] == order[None, :]).astype(BF)
    pan_low = mm(pan[:, tail:], swap).astype(BF)
    quarter = carried // 4
    inner = targets.reshape(-1)[carried - quarter:] - tail
    reach = (inner[:, None] == order[None, :]).astype(BF)

    coeffs = block_coeffs[0]
    base = mm(pan, eff)

    def mixed_of(cin):
        w = (base + mm(cin, gath)).astype(BF)
        return mm(w, coeffs).astype(BF)

    def advance(cin):
        m = mixed_of(cin)
        a = (pan_low.astype(F32) + mm(cin[:, carried - quarter:], reach)).astype(BF)
        return (a.astype(F32) - mm(m, low, ((1,), (1,)))).astype(BF)

    cin = jnp.zeros((part, carried), BF)
    for step in range(1, fronts):
        sent = advance(cin)
        came = lax.ppermute(sent, "front", [(step - 1, step)])
        cin = jnp.where(front == step, came, cin)

    m = mixed_of(cin)
    moved = lax.dot_general(
        cin.reshape(part, rows, each), pick, (((2,), (1,)), ((1,), (0,))), preferred_element_type=F32
    )
    a = (got.astype(F32) + moved).astype(BF)
    back = mm(m, eff, ((1,), (1,))).reshape(part, rows, span).transpose(1, 0, 2)
    out = (a.astype(F32) - back).astype(BF)
    home = lax.all_to_all(out, "row", 0, 0, tiled=True)
    return home.reshape(cols, span).T[None]


def solution(mesh):
    in_specs = (
        P("front", "row", None),
        P("front", "row", None),
        P("front", None, None),
        P("front", "row", None),
        P("front", None),
        P("front", None),
    )
    out_specs = P("front", "row", None)
    return jax.shard_map(local, mesh=mesh, in_specs=in_specs, out_specs=out_specs, check_vma=False)
```

time: 1820 us -> 140 us (0.08)
  blocking collectives: 1490 us -> 20.8 us
  starting transfers between devices: 136 us -> 13 us
  waiting for transfers between devices: 144 us -> 61.6 us
    psum x12 -> x0, blocking collectives: 1490 us -> none  [advance(): totals = lax.psum(partial_value, 'row')]
    all_to_all x12 -> x1, starting transfers between devices: 120 us -> 7.76 us  [local(): got = lax.all_to_all(pieces, 'row', 0, 0, tiled=True)]
    all_to_all x12 -> x1, waiting for transfers between devices: 89.4 us -> 7.38 us  [local(): got = lax.all_to_all(pieces, 'row', 0, 0, tiled=True)]
    ppermute x12 -> x7, waiting for transfers between devices: 54.3 us -> 22.7 us  [local(): came = lax.ppermute(sent, 'front', [(step - 1, step)])]
    all_gather x0 -> x1, waiting for transfers between devices: none -> 31.6 us  [local(): eff = lax.all_gather(own, 'row', axis=0, tiled=True)]
    all_to_all x0 -> x1, blocking collectives: none -> 20.8 us  [local(): home = lax.all_to_all(out, 'row', 0, 0, tiled=True)]
  transfers between devices with their start and end apart: 24 -> 9, of which waited for: 24 -> 3; matrix products, arithmetic and copies ran while one was open for 0% -> 4% of each run, Pallas kernels for 0% -> 0%
where the time goes in v1:
time: 140 us
  waiting for transfers between devices  61.6 us (44%)
  blocking collectives  20.8 us (15%)
  matrix products  19.7 us (14%)
  between operations  13.8 us (10%)
  starting transfers between devices  13 us (9%)
  local copies, waits for them, and re-layouts  7.13 us (5%)
  other arithmetic  3.85 us (3%)
    all_gather x1, waiting for transfers between devices, local(): eff = lax.all_gather(own, 'row', axis=0, tiled=True)  31.6 us
    ppermute x7, waiting for transfers between devices, local(): came = lax.ppermute(sent, 'front', [(step - 1, step)])  22.7 us
    all_to_all x1, blocking collectives, local(): home = lax.all_to_all(out, 'row', 0, 0, tiled=True)  20.8 us
    dot_general x25, matrix products, mm(): return lax.dot_general(a, b, (dims, ((), ())), preferred_element_type=F32)  18.4 us
    all_to_all x1, starting transfers between devices, local(): got = lax.all_to_all(pieces, 'row', 0, 0, tiled=True)  7.76 us
    all_to_all x1, waiting for transfers between devices, local(): got = lax.all_to_all(pieces, 'row', 0, 0, tiled=True)  7.38 us
    ppermute x7, starting transfers between devices, local(): came = lax.ppermute(sent, 'front', [(step - 1, step)])  5.29 us
  transfers between devices with their start and end apart: 9, of which 3 were waited for; matrix products, arithmetic and copies ran while one was open for 4% of the time, Pallas kernels for 0%

profile of v1, /device:TPU:225, one launch (start us, length us, event | category | flops | bytes accessed | tf_op | source)
XLA Modules:
  0.0 139.9 jit_solution(17026413127289061736)
XLA Ops:
  6.5 0.8 broadcast_bitcast_fusion
  8.1 1.7 %and_select_fusion = bf16[128,512]{1,0:T(8,128)(2,1)} fusion(bf16[1,128,512]{2,1,0:T(8,128)(2,1)} %param.7, s32[512]{0:T(512)S(1)} %broadcast_bitcast_fusion, s32[128]{0:T(128)S(1)} %iota_add_fusion, pred[512]{0:T(512)(128)(4,1)S(1)} %broadcast_bitcast_fusion.1), kind=kLoop, calls=%fused_computation.114 | loop fusion | flops 196608 | bytes 265216 | tf_op jit(solution)/shard_map/jit(_where)/select_n | solution.py:31
  9.8 1.9 %copy.17 = bf16[1280,128]{1,0:T(8,128)(2,1)} copy(bf16[1280,128]{0,1:T(8,128)(2,1)} %bitcast.127) | data formatting | bytes 655360 | tf_op jit(solution)/shard_map/transpose | solution.py:34
  11.6 7.8 %all-to-all-start = ((bf16[32,40,128]{2,1,0:T(8,128)(2,1)}), bf16[32,40,128]{2,1,0:T(8,128)(2,1)S(1)}, u32[]{:S(2)}, u32[]{:S(2)}) async-start(bf16[32,40,128]{2,1,0:T(8,128)(2,1)} %bitcast.2), calls=%async_computation | async-start | bytes 655360 | tf_op jit(solution)/shard_map/all_to_all | solution.py:35
  20.0 1.3 reduce.3
  21.6 7.4 %all-to-all-done = bf16[32,40,128]{2,1,0:T(8,128)(2,1)S(1)} async-done(((bf16[32,40,128]{2,1,0:T(8,128)(2,1)}), bf16[32,40,128]{2,1,0:T(8,128)(2,1)S(1)}, u32[]{:S(2)}, u32[]{:S(2)}) %all-to-all-start) | async-done | bytes 327712 | tf_op jit(solution)/shard_map/all_to_all | solution.py:35
  29.0 0.8 fusion.50
  30.2 31.6 %all-gather.2.cloned.1.call-done = bf16[4096,512]{1,0:T(8,128)(2,1)} async-done(((bf16[128,512]{1,0:T(8,128)(2,1)}), bf16[4096,512]{1,0:T(8,128)(2,1)}) %all-gather.2.cloned.1.call-update) | async-done | bytes 4194320 | tf_op jit(solution)/shard_map/all_gather | solution.py:32
  61.8 1.4 %slice.43 = bf16[1024,512]{1,0:T(8,128)(2,1)S(1)} slice(bf16[4096,512]{1,0:T(8,128)(2,1)} %all-gather.2.cloned.1.call-done), slice={[3072:4096], [0:512]} | slice | bytes 2097152 | tf_op jit(solution)/shard_map/slice | solution.py:44
  64.3 0.7 convolution_convert_fusion
  65.0 0.8 convolution_bitcast_fusion.1
  66.7 0.7 collective-permute-start
  68.6 0.7 collective-permute-start.1
  69.3 1.3 fusion.78
  71.4 0.7 collective-permute-start.2
  72.1 1.3 fusion.72
  75.0 1.3 fusion.66
  77.8 1.3 fusion.60
  80.6 1.3 fusion.54
  82.7 1.3 collective-permute-start.6
  84.1 22.6 %collective-permute-done.6 = bf16[40,1024]{1,0:T(8,128)(2,1)S(1)} collective-permute-done((bf16[40,1024]{1,0:T(8,128)(2,1)S(1)}, bf16[40,1024]{1,0:T(8,128)(2,1)S(1)}, u32[]{:S(2)}, u32[]{:S(2)}) %collective-permute-start.6) | collective-permute-done | bytes 81952 | tf_op jit(solution)/shard_map/ppermute | solution.py:67
  107.3 3.5 %convolution_bitcast_fusion = f32[5,32,8,128]{3,2,1,0:T(8,128)S(1)} fusion(bf16[40,512]{1,0:T(8,128)(2,1)S(1)} %convolution_convert_fusion.1, bf16[4096,512]{1,0:T(8,128)(2,1)} %all-gather.2.cloned.1.call-done), kind=kOutput, calls=%fused_computation.18 | convolution fusion | flops 167772160 | bytes 4890624 | tf_op jit(solution)/shard_map/dot_general | solution.py:12
  111.4 20.8 %all_to_all.10 = bf16[32,40,128]{2,1,0:T(8,128)(2,1)S(1)} all-to-all(bf16[32,40,128]{2,1,0:T(8,128)(2,1)S(1)} %fusion.19), channel_id=1, replica_groups=mesh['front'=8,'row'=32] {'row'}, dimensions={0} | all-to-all | bytes 655360 | tf_op jit(solution)/shard_map/all_to_all | solution.py:77
  132.2 0.9 copy.23
  (56 shorter events, 12.6 us)
Async XLA Ops:
  6.5 59.6 %copy-start = (bf16[1,512,512]{2,1,0:T(8,128)(2,1)S(1)}, bf16[1,512,512]{2,1,0:T(8,128)(2,1)}, u32[]{:S(2)}) copy-start(bf16[1,512,512]{2,1,0:T(8,128)(2,1)} %param.8) | copy-start | bytes 1572868
  6.5 55.2 %all-gather.2.cloned.1.call-start = ((), (), s32[]{:S(2)}) async-start(), calls=%async_computation.2 | async-start | bytes 4325376 | tf_op jit(solution)/shard_map/all_gather | solution.py:32
  11.6 17.4 %all-to-all-start = ((bf16[32,40,128]{2,1,0:T(8,128)(2,1)}), bf16[32,40,128]{2,1,0:T(8,128)(2,1)S(1)}, u32[]{:S(2)}, u32[]{:S(2)}) async-start(bf16[32,40,128]{2,1,0:T(8,128)(2,1)} %bitcast.2), calls=%async_computation | async-start | bytes 655360 | tf_op jit(solution)/shard_map/all_to_all | solution.py:35
  29.8 37.6 %copy-start.2 = (f32[40,1024]{1,0:T(8,128)}, f32[40,1024]{1,0:T(8,128)S(1)}, u32[]{:S(2)}) copy-start(f32[40,1024]{1,0:T(8,128)S(1)} %fusion.50) | copy-start | bytes 491524
  61.8 2.5 %copy-start.1 = (bf16[4096,512]{1,0:T(8,128)(2,1)S(1)}, bf16[4096,512]{1,0:T(8,128)(2,1)}, u32[]{:S(2)}) copy-start(bf16[4096,512]{1,0:T(8,128)(2,1)} %all-gather.2.cloned.1.call-done) | copy-start | bytes 12582916
  66.7 0.7 collective-permute-start
  68.6 0.7 collective-permute-start.1
  71.4 0.7 collective-permute-start.2
  74.3 0.7 collective-permute-start.3
  77.1 0.7 collective-permute-start.4
  79.9 0.7 collective-permute-start.5
  82.7 23.9 %collective-permute-start.6 = (bf16[40,1024]{1,0:T(8,128)(2,1)S(1)}, bf16[40,1024]{1,0:T(8,128)(2,1)S(1)}, u32[]{:S(2)}, u32[]{:S(2)}) collective-permute-start(bf16[40,1024]{1,0:T(8,128)(2,1)S(1)} %fusion.47), channel_id=1, source_target_pairs={{192,224},{193,225},{194,226},{195,227},{196,228},{197,229},{198,2... | collective-permute-start | bytes 245768 | tf_op jit(solution)/shard_map/ppermute | solution.py:67
Sparse Core Ops, SparseCore 0:
  9.9 51.8 all-gather.1
